TPU v7x, 256 devices: a whole 4x4x8 slice. The times are simulated.
256 devices in a mesh: pipe: 2 (over core), slab: 8 (over x, z_hi), dp: 16 (over z_lo, y).
Axes of the slice: x: 4, y: 4, z: 8 (z_hi: 2, z_lo: 4; z = z_hi * 4 + z_lo), core: 2. Of those that a mesh axis runs over, the one named last changes fastest.
Arguments:
- saved_inputs: bfloat16 [2, 2, 16, 2, 16, 16, 512], P('pipe', None, 'dp', None, 'slab'), may hold values from -12 to 12
- loss_cotangent: bfloat16 [2, 16, 2, 16, 16, 512], P(None, 'dp', None, 'slab'), may hold values from -3 to 3
- upstream: bfloat16 [16, 2, 16, 16, 512], P('dp', None, 'slab'), may hold values from -3 to 3
- conv_weight: bfloat16 [2, 512, 13824], P('pipe', 'dp'), may hold values from -0.0546875 to 0.0546875
- adagn_table: bfloat16 [2, 1000, 1024], P('pipe'), may hold values from -3 to 3
- timesteps: int32 [3, 16], P(None, 'dp'), may hold values from 0 to 999
- frame_counts: int32 [3, 16], P(None, 'dp'), may hold values from 1 to 2
Outputs:
- input_grads: bfloat16 [2, 2, 16, 2, 16, 16, 512], P('pipe', None, 'dp', None, 'slab')
- weight_grad: float32 [2, 512, 13824], P('pipe', 'dp')
- embed_grad: float32 [2, 2, 16, 1024], P('pipe', None, 'dp')
All inputs are finite; a program needn't handle non-finite values.
Results may differ from a plain program's by a relative error of at most 0.015.
Values may be sent and summed in bfloat16 or wider, within the bound.
A program may use at most 128 MiB of HBM per device.

v0:
```python
import math
import jax
import jax.numpy as jnp
from jax import lax
from jax.sharding import PartitionSpec as P

GROUPS = 32
EPS = 1e-05


def extended(x, sides, width):
    for axis, dim in sides:
        devices, length = (lax.axis_size(axis), x.shape[dim])
        up = [(i, (i + 1) % devices) for i in range(devices - 1)]
        down = [(j, i) for i, j in up]
        last = lax.slice_in_dim(x, length - width, length, axis=dim)
        initial = lax.slice_in_dim(x, 0, width, axis=dim)
        before = lax.ppermute(last, axis, up)
        after = lax.ppermute(initial, axis, down)
        x = jnp.concatenate([before, x, after], axis=dim)
    return x


def shifted(block, axis, distance):
    devices = range(lax.axis_size(axis))
    route = [(i - distance, i) for i in devices if i - distance in devices]
    return lax.ppermute(block, axis, route)


def group_sums(values, groups):
    summed = jnp.sum(values.reshape(-1, values.shape[-1]), axis=0)
    return jnp.sum(summed.reshape(groups, -1), axis=1)


def silu_grad(preact):
    sigma = jax.nn.sigmoid(preact)
    return sigma * (1.0 + preact * (1.0 - sigma))


def hidden_of(values, mean_c, rstd_c, gain_row, bias_row, mask_now):
    normed = (values - mean_c) * rstd_c
    preact = normed * gain_row + bias_row
    activated = jax.nn.silu(preact) * mask_now[:, None, None, None]
    return (normed, preact, activated)


def norm_terms(moment_one, moment_two, count_now):
    mean_g = moment_one / count_now
    var_g = moment_two / count_now - mean_g * mean_g
    return (mean_g, lax.rsqrt(var_g + EPS))


def tap_stack(padded, frames, slab_rows, cells_wide, mirrored):
    slices = []
    for depth_at in range(3):
        for vertical in range(3):
            for across in range(3):
                if mirrored:
                    offsets = (2 - depth_at, 2 - vertical, 2 - across)
                else:
                    offsets = (depth_at, vertical, across)
                slices.append(
                    padded[
                        ...,
                        offsets[0] : offsets[0] + frames,
                        offsets[1] : offsets[1] + slab_rows,
                        offsets[2] : offsets[2] + cells_wide,
                        :,
                    ]
                )
    return jnp.stack(slices, 0)


def pad_cells(values):
    return jnp.pad(values, ((1, 1), (0, 0), (1, 1), (0, 0)))


def local(
    saved_inputs, loss_cotangent, upstream, conv_weight, adagn_table, timesteps, frame_counts
):
    section_index = lax.axis_index("pipe")
    slab_count = lax.axis_size("slab")
    replicas = lax.axis_size("dp")
    inputs = saved_inputs[0, :, 0]
    tick_count, frames, slab_rows, cells_wide, channels = inputs.shape
    groups = GROUPS
    per_group = channels // groups
    height_total = slab_rows * slab_count
    step_table = adagn_table[0]
    weight_local = conv_weight[0]
    steps_now = lax.dynamic_slice_in_dim(timesteps[:, 0], section_index, tick_count)
    counts_now = lax.dynamic_slice_in_dim(frame_counts[:, 0], section_index, tick_count)
    onehot = (
        steps_now[:, None] == jnp.arange(step_table.shape[0], dtype=jnp.int32)[None, :]
    ).astype(jnp.bfloat16)
    embedded = jnp.dot(onehot, step_table, preferred_element_type=jnp.float32)
    scales = 1.0 + embedded[:, :channels]
    shifts = embedded[:, channels:]
    frame_masks = (jnp.arange(frames, dtype=jnp.int32)[None, :] < counts_now[:, None]).astype(
        jnp.float32
    )
    valid_counts = counts_now.astype(jnp.float32) * float(height_total * cells_wide * per_group)
    weight_norm = 1.0 / math.sqrt(tick_count * replicas * frames * height_total * cells_wide)
    embed_norm = 1.0 / math.sqrt(frames * height_total * cells_wide)
    full_weight = lax.all_gather(weight_local, "dp", axis=0, tiled=True).reshape(
        channels, 27, channels
    )
    dx_list = []
    embed_list = []
    hidden_exts = []
    cotangents = []
    received = None
    for tick_index in range(tick_count):
        values = inputs[tick_index].astype(jnp.float32)
        masked = values * frame_masks[tick_index][:, None, None, None]
        part_one = group_sums(masked, groups)
        part_two = group_sums(masked * values, groups)
        moment_one, moment_two = lax.psum((part_one, part_two), "slab")
        count_now = valid_counts[tick_index]
        mean_g, rstd_g = norm_terms(moment_one, moment_two, count_now)
        mean_c = jnp.repeat(mean_g, per_group)
        rstd_c = jnp.repeat(rstd_g, per_group)
        mask_now = frame_masks[tick_index]
        normed, preact, activated = hidden_of(
            inputs[tick_index].astype(jnp.float32),
            mean_c,
            rstd_c,
            scales[tick_index],
            shifts[tick_index],
            mask_now,
        )
        hidden_ext = extended(activated.astype(jnp.bfloat16), (("slab", 1),), 1)
        hidden_exts.append(hidden_ext)
        incoming = upstream[0] if tick_index == 0 else received
        cotangent = jnp.where(section_index == 1, loss_cotangent[tick_index, 0], incoming)
        cot_rows = extended(cotangent, (("slab", 1),), 1)
        cot_pad = pad_cells(cot_rows)
        tap_slices = tap_stack(cot_pad, frames, slab_rows, cells_wide, True)
        upward = jnp.einsum(
            "tfrwo,oti->frwi", tap_slices, full_weight, preferred_element_type=jnp.float32
        )
        pre_grad = upward * silu_grad(preact) * mask_now[:, None, None, None]
        dnormed = pre_grad * scales[tick_index]
        part_a = group_sums(dnormed, groups)
        part_b = group_sums(dnormed * normed, groups)
        scale_part = jnp.sum(pre_grad * normed, axis=(0, 1, 2))
        shift_part = jnp.sum(pre_grad, axis=(0, 1, 2))
        sum_a, sum_b, scale_sum, shift_sum = lax.psum(
            (part_a, part_b, scale_part, shift_part), "slab"
        )
        branch = (
            rstd_c
            * (
                dnormed
                - jnp.repeat(sum_a / count_now, per_group)
                - normed * jnp.repeat(sum_b / count_now, per_group)
            )
            * mask_now[:, None, None, None]
        )
        result = (cotangent.astype(jnp.float32) + branch).astype(jnp.bfloat16)
        dx_list.append(result)
        embed_list.append(jnp.concatenate([scale_sum, shift_sum]) * embed_norm)
        cotangents.append(cotangent)
        if tick_index + 1 < tick_count:
            received = shifted(result, "pipe", -1)
    cot_all = jnp.stack(cotangents)
    shard_rows = weight_local.shape[0]
    hidden_all = jnp.stack([pad_cells(one_ext) for one_ext in hidden_exts])
    hidden_taps = tap_stack(hidden_all, frames, slab_rows, cells_wide, False)
    grad_term = jnp.einsum(
        "kfrwo,tkfrwi->oti", cot_all, hidden_taps, preferred_element_type=jnp.float32
    )
    grad_shard = lax.psum_scatter(
        (grad_term.reshape(lax.axis_size("dp") * shard_rows, -1) * weight_norm).astype(
            jnp.bfloat16
        ),
        "dp",
        scatter_dimension=0,
        tiled=True,
    ).astype(jnp.float32)
    weight_grad = lax.psum(grad_shard, "slab")
    input_grads = jnp.stack(dx_list)[None, :, None]
    embed_grad = jnp.stack(embed_list)[None, :, None]
    return (input_grads, weight_grad[None], embed_grad)


def solution(mesh):
    placed = (
        P("pipe", None, "dp", None, "slab", None, None),
        P(None, "dp", None, "slab", None, None),
        P("dp", None, "slab", None, None),
        P("pipe", "dp", None),
        P("pipe", None, None),
        P(None, "dp"),
        P(None, "dp"),
    )
    return jax.shard_map(
        local,
        mesh=mesh,
        in_specs=placed,
        out_specs=(
            P("pipe", None, "dp", None, "slab", None, None),
            P("pipe", "dp", None),
            P("pipe", None, "dp", None),
        ),
        check_vma=False,
    )
```

profile of v0, /device:TPU:8, one launch (start us, length us, event | category | flops | bytes accessed | tf_op | source)
XLA Modules:
  0.0 686.2 jit_solution(7426702432679894269)
XLA Ops:
  7.2 0.7 all-gather.3.cloned.1.call-update
  8.0 0.9 bitcast_select_fusion.2
  8.9 9.1 %collective-permute-start = (bf16[2,1,16,512]{3,2,1,0:T(8,128)(2,1)S(1)}, bf16[2,1,16,512]{3,2,1,0:T(8,128)(2,1)S(1)}, u32[]{:S(2)}, u32[]{:S(2)}) collective-permute-start(bf16[2,1,16,512]{3,2,1,0:T(8,128)(2,1)S(1)} %get-tuple-element.56), channel_id=1, source_target_pairs={{0,16},{16,32},{32,48},{48,64},{64,80},{80,96},{96,112},{1,17},{17... | collective-permute-start | bytes 98312 | tf_op jit(solution)/shard_map/ppermute | solution.py:18
  18.0 1.3 collective-permute-start.1
  19.3 0.7 convert_multiply_fusion.4
  20.1 1.0 fusion.43
  21.5 32.6 %all-reduce.6 = (f32[32]{0:T(128)S(1)}, f32[32]{0:T(128)S(1)}) all-reduce(f32[32]{0:T(128)S(1)} %reduce_sum.183, f32[32]{0:T(128)S(1)} %reduce_sum.181), channel_id=1, replica_groups=mesh['pipe'=2,'slab'=8,'dp'=16] {'slab'}, use_global_device_ids=true, to_apply=%region_5.0 | all-reduce | flops 64 | bytes 512 | tf_op jit(solution)/shard_map/psum | solution.py:118
  54.1 0.7 dynamic-slice_bitcast_fusion
  55.9 0.7 add_rsqrt_fusion.1
  57.3 0.7 constant_dynamic-update-slice_fusion.26
  58.0 0.6 constant_dynamic-update-slice_fusion.25
  58.6 0.6 constant_dynamic-update-slice_fusion.24
  59.3 0.6 constant_dynamic-update-slice_fusion.23
  59.9 0.6 constant_dynamic-update-slice_fusion.22
  60.6 0.6 constant_dynamic-update-slice_fusion.21
  61.2 0.6 constant_dynamic-update-slice_fusion.20
  61.9 0.6 constant_dynamic-update-slice_fusion.19
  62.5 0.6 constant_dynamic-update-slice_fusion.18
  63.1 0.6 constant_dynamic-update-slice_fusion.17
  63.8 0.6 constant_dynamic-update-slice_fusion.16
  64.4 0.6 constant_dynamic-update-slice_fusion.15
  65.1 0.6 constant_dynamic-update-slice_fusion.14
  65.7 0.6 constant_dynamic-update-slice_fusion.13
  66.4 0.6 constant_dynamic-update-slice_fusion.12
  67.0 0.6 constant_dynamic-update-slice_fusion.11
  67.7 0.6 constant_dynamic-update-slice_fusion.10
  68.3 0.6 constant_dynamic-update-slice_fusion.9
  68.9 0.6 constant_dynamic-update-slice_fusion.8
  69.6 0.6 constant_dynamic-update-slice_fusion.7
  70.2 0.6 constant_dynamic-update-slice_fusion.6
  70.9 0.6 constant_dynamic-update-slice_fusion.5
  71.5 0.6 constant_dynamic-update-slice_fusion.4
  72.2 0.6 constant_dynamic-update-slice_fusion.3
  72.8 0.6 constant_dynamic-update-slice_fusion.2
  73.4 0.6 constant_dynamic-update-slice_fusion.1
  74.1 0.6 constant_dynamic-update-slice_fusion
  74.7 94.1 %all-gather.3.cloned.1.call-done = bf16[1,512,13824]{2,1,0:T(8,128)(2,1)} async-done(((bf16[1,32,13824]{2,1,0:T(8,128)(2,1)}), bf16[1,512,13824]{2,1,0:T(8,128)(2,1)}) %all-gather.3.cloned.1.call-update) | async-done | bytes 14155792 | tf_op jit(solution)/shard_map/all_gather | solution.py:105
  168.8 18.7 %copy.101 = bf16[1,512,13824]{1,2,0:T(8,128)(2,1)} copy(bf16[1,512,13824]{2,1,0:T(8,128)(2,1)} %all-gather.3.cloned.1.call-done) | data formatting | bytes 28311552 | tf_op jit(solution)/shard_map/all_gather | solution.py:105
  187.5 10.0 %fusion.42 = (f32[512]{0:T(512)S(1)}, f32[512]{0:T(512)S(1)}, f32[512]{0:T(512)S(1)}, f32[512]{0:T(512)S(1)}, f32[2,2,16,512]{3,2,1,0:T(8,128)S(1)}) fusion(f32[512]{0:T(512)S(1)} %sub.59, f32[512]{0:T(512)S(1)} %mul.241, bf16[1,2,1,2,2,16,512]{6,5,4,3,2,1,0:T(8,128)(2,1)S(1)} %copy-done.3, f32[512]{0:T(512)S(1)} %bitcast.570, ...), kind=kOutput, calls=%fused_computation.194 | convolution fusion | flops 906655744 | bytes 16138248 | tf_op jit(solution)/shard_map/tfrwo,oti->frwi/dot_general | solution.py:139
  197.9 31.7 %all-reduce.5 = (f32[32]{0:T(128)S(1)}, f32[32]{0:T(128)S(1)}, f32[32]{0:T(128)S(1)}, f32[32]{0:T(128)S(1)}) all-reduce(f32[32]{0:T(128)S(1)} %reduce_sum.187, f32[32]{0:T(128)S(1)} %reduce_sum.185, f32[32]{0:T(128)S(1)} %reduce_sum.191, f32[32]{0:T(128)S(1)} %reduce_sum.189), channel_id=1, replica_groups=mesh['pipe'=2,'slab'=8,'dp'=16] {'slab'}, use_global_device_ids=true, to_apply=%region_11.12 | all-reduce | flops 128 | bytes 1024 | tf_op jit(solution)/shard_map/psum | solution.py:148
  229.6 0.6 broadcast_divide_fusion.3
  230.7 1.3 collective-permute-start.2
  232.0 1.8 collective-permute-done.2
  233.8 1.3 collective-permute-start.3
  235.1 1.3 collective-permute-start.4
  236.4 0.7 add_rsqrt_fusion
  237.4 8.5 %collective-permute-start.5 = (bf16[2,1,16,512]{3,2,1,0:T(8,128)(2,1)S(1)}, bf16[2,1,16,512]{3,2,1,0:T(8,128)(2,1)S(1)}, u32[]{:S(2)}, u32[]{:S(2)}) collective-permute-start(bf16[2,1,16,512]{3,2,1,0:T(8,128)(2,1)S(1)} %get-tuple-element.52), channel_id=1, source_target_pairs={{0,16},{16,32},{32,48},{48,64},{64,80},{80,96},{96,112},{1,17},{17... | collective-permute-start | bytes 98312 | tf_op jit(solution)/shard_map/ppermute | solution.py:18
  245.9 1.3 collective-permute-start.6
  247.9 9.4 %fusion.6 = f32[2,2,16,512]{3,2,0,1:T(8,128)S(1)} fusion(bf16[512,27,512,1,1]{0,2,3,4,1:T(8,128)(2,1)} %bitcast.562, bf16[27,2,2,16,512]{4,3,2,1,0:T(8,128)(2,1)S(1)} %constant_dynamic-update-slice_fusion.27), kind=kOutput, calls=%fused_computation.63 | convolution fusion | flops 905969664 | bytes 16056320 | tf_op jit(solution)/shard_map/tfrwo,oti->frwi/dot_general | solution.py:139
  257.5 8.7 %collective-permute-start.7 = (bf16[2,1,16,512]{3,2,1,0:T(8,128)(2,1)S(1)}, bf16[2,1,16,512]{3,2,1,0:T(8,128)(2,1)S(1)}, u32[]{:S(2)}, u32[]{:S(2)}) collective-permute-start(bf16[2,1,16,512]{3,2,1,0:T(8,128)(2,1)S(1)} %get-tuple-element.50), channel_id=1, source_target_pairs={{0,16},{16,32},{32,48},{48,64},{64,80},{80,96},{96,112},{1,17},{17... | collective-permute-start | bytes 98312 | tf_op jit(solution)/shard_map/ppermute | solution.py:18
  266.2 1.3 collective-permute-start.8
  267.8 9.0 %collective-permute-done.8 = bf16[2,1,16,512]{3,2,1,0:T(8,128)(2,1)S(1)} collective-permute-done((bf16[2,1,16,512]{3,2,1,0:T(8,128)(2,1)S(1)}, bf16[2,1,16,512]{3,2,1,0:T(8,128)(2,1)S(1)}, u32[]{:S(2)}, u32[]{:S(2)}) %collective-permute-start.8) | collective-permute-done | bytes 32800 | tf_op jit(solution)/shard_map/ppermute | solution.py:19
  278.0 1.7 copy-done.2
  279.7 9.1 %fusion = bf16[512,27,512]{0,2,1:T(8,128)(2,1)} fusion(bf16[27,2,2,2,16,512]{5,4,3,2,1,0:T(8,128)(2,1)} %copy-done.2, bf16[1,2,2,16,512]{4,3,2,1,0:T(8,128)(2,1)S(1)} %bitcast.564, bf16[1,2,2,16,512]{4,3,2,1,0:T(8,128)(2,1)S(1)} %get-tuple-element.46), kind=kOutput, calls=%fused_computation.1 | convolution fusion | flops 1826160640 | bytes 17825792 | tf_op jit(solution)/shard_map/kfrwo,tkfrwi->oti/dot_general | solution.py:170
  288.8 18.6 %copy.108 = bf16[512,13824]{1,0:T(8,128)(2,1)} copy(bf16[512,13824]{0,1:T(8,128)(2,1)} %bitcast.563) | data formatting | bytes 28311552 | tf_op jit(solution)/shard_map/convert_element_type | solution.py:174
  307.5 193.0 %reduce-scatter.2.cloned.1.call-done = bf16[32,13824]{1,0:T(8,128)(2,1)} async-done(((bf16[512,13824]{1,0:T(8,128)(2,1)}), bf16[32,13824]{1,0:T(8,128)(2,1)}) %reduce-scatter.2.cloned.1.call-update) | async-done | bytes 884752 | tf_op jit(solution)/shard_map/reduce_scatter | solution.py:173
  500.5 2.5 bitcast_convert_fusion
  503.5 35.7 %all-reduce.4 = (f32[32]{0:T(128)S(1)}, f32[32]{0:T(128)S(1)}, f32[1,512]{1,0:T(1,128)S(1)}, f32[1,512]{1,0:T(1,128)S(1)}, f32[1,512]{1,0:T(1,128)S(1)}, /*index=5*/f32[1,512]{1,0:T(1,128)S(1)}) all-reduce(f32[32]{0:T(128)S(1)} %reduce_sum.195, f32[32]{0:T(128)S(1)} %reduce_sum.193, ...), channel_id=1, replica_groups=mesh['pipe'=2,'slab'=8,'dp'=16] {'slab'}, use_global_device_ids=true, to_apply=%region_23.24 | all-reduce | flops 2112 | bytes 16896 | tf_op jit(solution)/shard_map/psum | solution.py:148
  539.2 0.6 broadcast_in_dim.47
  539.8 0.6 broadcast_divide_fusion.1
  540.6 0.7 broadcast_divide_fusion
  541.5 0.7 maximum_bitcast_fusion
  542.2 134.7 %all-reduce.9.cloned.1.call-done = f32[1,32,13824]{2,1,0:T(8,128)} async-done(((f32[1,32,13824]{2,1,0:T(8,128)}), f32[1,32,13824]{2,1,0:T(8,128)}) %all-reduce.9.cloned.1.call-update) | async-done | bytes 1769488 | tf_op jit(solution)/shard_map/psum | solution.py:181
  676.9 2.8 copy.209
  (131 shorter events, 6.2 us)
Async XLA Ops:
  7.2 48.2 %copy-start = (bf16[1,1000,1024]{2,1,0:T(8,128)(2,1)S(1)}, bf16[1,1000,1024]{2,1,0:T(8,128)(2,1)}, u32[]{:S(2)}) copy-start(bf16[1,1000,1024]{2,1,0:T(8,128)(2,1)} %param.11) | copy-start | bytes 6144004
  7.2 161.6 %all-gather.3.cloned.1.call-start = ((), (), s32[]{:S(2)}) async-start(), calls=%async_computation.3 | async-start | bytes 15040512 | tf_op jit(solution)/shard_map/all_gather | solution.py:105
  7.9 492.6 %reduce-scatter.2.cloned.1.call-start = ((), (), s32[]{:S(2)}) async-start(), calls=%async_computation.1 | async-start | bytes 15040512 | tf_op jit(solution)/shard_map/reduce_scatter | solution.py:173
  8.9 48.4 %collective-permute-start = (bf16[2,1,16,512]{3,2,1,0:T(8,128)(2,1)S(1)}, bf16[2,1,16,512]{3,2,1,0:T(8,128)(2,1)S(1)}, u32[]{:S(2)}, u32[]{:S(2)}) collective-permute-start(bf16[2,1,16,512]{3,2,1,0:T(8,128)(2,1)S(1)} %get-tuple-element.56), channel_id=1, source_target_pairs={{0,16},{16,32},{32,48},{48,64},{64,80},{80,96},{96,112},{1,17},{17... | collective-permute-start | bytes 98312 | tf_op jit(solution)/shard_map/ppermute | solution.py:18
  18.0 39.3 %collective-permute-start.1 = (bf16[2,1,16,512]{3,2,1,0:T(8,128)(2,1)S(1)}, bf16[2,1,16,512]{3,2,1,0:T(8,128)(2,1)S(1)}, u32[]{:S(2)}, u32[]{:S(2)}) collective-permute-start(bf16[2,1,16,512]{3,2,1,0:T(8,128)(2,1)S(1)} %get-tuple-element.57), channel_id=1, source_target_pairs={{16,0},{32,16},{48,32},{64,48},{80,64},{96,80},{112,96},{17,1},{33... | collective-permute-start | bytes 98312 | tf_op jit(solution)/shard_map/ppermute | solution.py:19
  55.4 10.3 %copy-start.4 = (bf16[2,1,2,2,16,512]{5,4,3,2,1,0:T(8,128)(2,1)S(1)}, bf16[2,1,2,2,16,512]{5,4,3,2,1,0:T(8,128)(2,1)}, u32[]{:S(2)}) copy-start(bf16[2,1,2,2,16,512]{5,4,3,2,1,0:T(8,128)(2,1)} %param.8) | copy-start | bytes 393220
  55.4 10.3 %copy-start.5 = (bf16[1,2,2,16,512]{4,3,2,1,0:T(8,128)(2,1)S(1)}, bf16[1,2,2,16,512]{4,3,2,1,0:T(8,128)(2,1)}, u32[]{:S(2)}) copy-start(bf16[1,2,2,16,512]{4,3,2,1,0:T(8,128)(2,1)} %param.9) | copy-start | bytes 196612
  74.7 112.8 %copy-start.3 = (bf16[1,2,1,2,2,16,512]{6,5,4,3,2,1,0:T(8,128)(2,1)S(1)}, bf16[1,2,1,2,2,16,512]{6,5,4,3,2,1,0:T(8,128)(2,1)}, u32[]{:S(2)}) copy-start(bf16[1,2,1,2,2,16,512]{6,5,4,3,2,1,0:T(8,128)(2,1)} %param.7) | copy-start | bytes 393220
  230.7 3.1 collective-permute-start.2
  233.8 13.3 %collective-permute-start.3 = (bf16[2,1,16,512]{3,2,1,0:T(8,128)(2,1)S(1)}, bf16[2,1,16,512]{3,2,1,0:T(8,128)(2,1)S(1)}, u32[]{:S(2)}, u32[]{:S(2)}) collective-permute-start(bf16[2,1,16,512]{3,2,1,0:T(8,128)(2,1)S(1)} %get-tuple-element.54), channel_id=1, source_target_pairs={{0,16},{16,32},{32,48},{48,64},{64,80},{80,96},{96,112},{1,17},{17... | collective-permute-start | bytes 98312 | tf_op jit(solution)/shard_map/ppermute | solution.py:18
  235.1 12.0 %collective-permute-start.4 = (bf16[2,1,16,512]{3,2,1,0:T(8,128)(2,1)S(1)}, bf16[2,1,16,512]{3,2,1,0:T(8,128)(2,1)S(1)}, u32[]{:S(2)}, u32[]{:S(2)}) collective-permute-start(bf16[2,1,16,512]{3,2,1,0:T(8,128)(2,1)S(1)} %get-tuple-element.55), channel_id=1, source_target_pairs={{16,0},{32,16},{48,32},{64,48},{80,64},{96,80},{112,96},{17,1},{33... | collective-permute-start | bytes 98312 | tf_op jit(solution)/shard_map/ppermute | solution.py:19
  237.4 30.1 %collective-permute-start.5 = (bf16[2,1,16,512]{3,2,1,0:T(8,128)(2,1)S(1)}, bf16[2,1,16,512]{3,2,1,0:T(8,128)(2,1)S(1)}, u32[]{:S(2)}, u32[]{:S(2)}) collective-permute-start(bf16[2,1,16,512]{3,2,1,0:T(8,128)(2,1)S(1)} %get-tuple-element.52), channel_id=1, source_target_pairs={{0,16},{16,32},{32,48},{48,64},{64,80},{80,96},{96,112},{1,17},{17... | collective-permute-start | bytes 98312 | tf_op jit(solution)/shard_map/ppermute | solution.py:18
  245.9 21.6 %collective-permute-start.6 = (bf16[2,1,16,512]{3,2,1,0:T(8,128)(2,1)S(1)}, bf16[2,1,16,512]{3,2,1,0:T(8,128)(2,1)S(1)}, u32[]{:S(2)}, u32[]{:S(2)}) collective-permute-start(bf16[2,1,16,512]{3,2,1,0:T(8,128)(2,1)S(1)} %get-tuple-element.53), channel_id=1, source_target_pairs={{16,0},{32,16},{48,32},{64,48},{80,64},{96,80},{112,96},{17,1},{33... | collective-permute-start | bytes 98312 | tf_op jit(solution)/shard_map/ppermute | solution.py:19
  257.5 10.3 %collective-permute-start.7 = (bf16[2,1,16,512]{3,2,1,0:T(8,128)(2,1)S(1)}, bf16[2,1,16,512]{3,2,1,0:T(8,128)(2,1)S(1)}, u32[]{:S(2)}, u32[]{:S(2)}) collective-permute-start(bf16[2,1,16,512]{3,2,1,0:T(8,128)(2,1)S(1)} %get-tuple-element.50), channel_id=1, source_target_pairs={{0,16},{16,32},{32,48},{48,64},{64,80},{80,96},{96,112},{1,17},{17... | collective-permute-start | bytes 98312 | tf_op jit(solution)/shard_map/ppermute | solution.py:18
  266.2 10.6 %collective-permute-start.8 = (bf16[2,1,16,512]{3,2,1,0:T(8,128)(2,1)S(1)}, bf16[2,1,16,512]{3,2,1,0:T(8,128)(2,1)S(1)}, u32[]{:S(2)}, u32[]{:S(2)}) collective-permute-start(bf16[2,1,16,512]{3,2,1,0:T(8,128)(2,1)S(1)} %get-tuple-element.51), channel_id=1, source_target_pairs={{16,0},{32,16},{48,32},{64,48},{80,64},{96,80},{112,96},{17,1},{33... | collective-permute-start | bytes 98312 | tf_op jit(solution)/shard_map/ppermute | solution.py:19
  278.0 1.7 copy-start.2
  307.5 369.4 %all-reduce.9.cloned.1.call-start = ((), (), s32[]{:S(2)}) async-start(), calls=%async_computation.2 | async-start | bytes 3538944 | tf_op jit(solution)/shard_map/psum | solution.py:181
  541.5 138.2 %copy-start.1 = (bf16[1,1000,1024]{2,1,0:T(8,128)(2,1)S(1)}, bf16[1,1000,1024]{2,1,0:T(8,128)(2,1)}, u32[]{:S(2)}) copy-start(bf16[1,1000,1024]{2,1,0:T(8,128)(2,1)} %param.11) | copy-start | bytes 6144004
Sparse Core Ops, SparseCore 0:
  9.8 158.9 all-gather.2
  307.6 192.8 reduce-scatter.1
  503.8 173.0 all-reduce.8
where the time goes:
time: 688 us; the launch traced here: 686 us
  waiting for transfers between devices  434 us (63%)
  blocking collectives  100 us (15%)
  local copies, waits for them, and re-layouts  61.5 us (9%)
  starting transfers between devices  34.2 us (5%)
  matrix products  28.9 us (4%)
  between operations  14.6 us (2%)
  other arithmetic  13.5 us (2%)
    reduce_scatter x1, waiting for transfers between devices, local(): lax.psum_scatter((grad_term.reshape(lax.axis_size('dp') * shard_rows, -1)...  193 us
    psum x1, waiting for transfers between devices, local(): weight_grad = lax.psum(grad_shard, 'slab')  135 us
    all_gather x1, waiting for transfers between devices, local(): lax.all_gather(weight_local, 'dp', axis=0, tiled=True)  94.1 us
    psum x2, blocking collectives, local(): lax.psum((part_a, part_b, scale_part, shift_part), 'slab')  67.4 us
    psum x1, blocking collectives, local(): moment_one, moment_two = lax.psum((part_one, part_two), 'slab')  32.6 us
    ppermute x4, starting transfers between devices, extended(): before = lax.ppermute(last, axis, up)  27.6 us
    unnamed x60, local copies, waits for them, and re-layouts  19.8 us
    dot_general x2, matrix products, local(): jnp.einsum('tfrwo,oti->frwi', tap_slices, full_weight, preferred_element_...  19.4 us
  transfers between devices with their start and end apart: 12, of which 6 were waited for; matrix products, arithmetic and copies ran while one was open for 6% of the time, Pallas kernels for 0%

commit v1 on v0

--- a/solution.py
+++ b/solution.py
@@ -1,3 +1,4 @@
+import functools
 import math
 import jax
 import jax.numpy as jnp
@@ -6,6 +7,15 @@
 
 GROUPS = 32
 EPS = 1e-05
+
+
+def regions_solve(frame_in, array_axis):
+    x_next = jnp.stack([frame_in for _ in range(lax.axis_size("dp"))])
+    carry_in = lax.all_to_all(x_next, concat_axis=0, split_axis=0, axis_name="dp")
+    return jnp.concatenate(carry_in, axis=array_axis)
+
+
+_map_words = functools.partial(regions_solve, array_axis=0)
 
 
 def extended(x, sides, width):
@@ -102,9 +112,7 @@
     valid_counts = counts_now.astype(jnp.float32) * float(height_total * cells_wide * per_group)
     weight_norm = 1.0 / math.sqrt(tick_count * replicas * frames * height_total * cells_wide)
     embed_norm = 1.0 / math.sqrt(frames * height_total * cells_wide)
-    full_weight = lax.all_gather(weight_local, "dp", axis=0, tiled=True).reshape(
-        channels, 27, channels
-    )
+    full_weight = _map_words(weight_local).reshape(channels, 27, channels)
     dx_list = []
     embed_list = []
     hidden_exts = []

time: 688 us -> 848 us (1.23)
  blocking collectives: 100 us -> 308 us
  waiting for transfers between devices: 434 us -> 341 us
  matrix products: 28.9 us -> 58 us
  local copies, waits for them, and re-layouts: 61.5 us -> 71 us
  starting transfers between devices: 34.2 us -> 42.7 us
    psum x1, blocking collectives: 32.6 us -> 244 us  [local(): moment_one, moment_two = lax.psum((part_one, part_two), 'slab')]
    all_gather x1 -> x0, waiting for transfers between devices: 94.1 us -> none  [local(): lax.all_gather(weight_local, 'dp', axis=0, tiled=True)]
    dot_general x2, matrix products: 19.4 us -> 48.5 us  [local(): jnp.einsum('tfrwo,oti->frwi', tap_slices, full_weight, preferred_element_...]
    another operation x0 -> x2, local copies, waits for them, and re-layouts: none -> 28.8 us  [the longest x1 21.1 us: local(): full_weight = _map_words(weight_local).reshape(channels, 27, channels)]
    all_gather x1 -> x0, local copies, waits for them, and re-layouts: 18.7 us -> none  [local(): lax.all_gather(weight_local, 'dp', axis=0, tiled=True)]
    all_to_all x0 -> x1, starting transfers between devices: none -> 9.14 us  [regions_solve(): lax.all_to_all(x_next, concat_axis=0, split_axis=0, axis_name='dp')]
    unnamed x60 -> x64, local copies, waits for them, and re-layouts: 19.8 us -> 19.8 us
  transfers between devices with their start and end apart: 12 -> 12, of which waited for: 6 -> 4; matrix products, arithmetic and copies ran while one was open for 6% -> 6% of each run, Pallas kernels for 0% -> 0%
where the time goes in v1:
time: 848 us; the launch traced here: 847 us
  waiting for transfers between devices  341 us (40%)
  blocking collectives  308 us (36%)
  local copies, waits for them, and re-layouts  71 us (8%)
  matrix products  58 us (7%)
  starting transfers between devices  42.7 us (5%)
  between operations  14.9 us (2%)
  other arithmetic  11.1 us (1%)
    psum x1, blocking collectives, local(): moment_one, moment_two = lax.psum((part_one, part_two), 'slab')  244 us
    reduce_scatter x1, waiting for transfers between devices, local(): lax.psum_scatter((grad_term.reshape(lax.axis_size('dp') * shard_rows, -1)...  196 us
    psum x1, waiting for transfers between devices, local(): weight_grad = lax.psum(grad_shard, 'slab')  135 us
    psum x2, blocking collectives, local(): lax.psum((part_a, part_b, scale_part, shift_part), 'slab')  64.1 us
    dot_general x2, matrix products, local(): jnp.einsum('tfrwo,oti->frwi', tap_slices, full_weight, preferred_element_...  48.5 us
    ppermute x4, starting transfers between devices, extended(): before = lax.ppermute(last, axis, up)  26.6 us
    another operation x1, local copies, waits for them, and re-layouts, local(): full_weight = _map_words(weight_local).reshape(channels, 27, channels)  21.1 us
    unnamed x64, local copies, waits for them, and re-layouts  19.8 us
  transfers between devices with their start and end apart: 12, of which 4 were waited for; matrix products, arithmetic and copies ran while one was open for 6% of the time, Pallas kernels for 0%

profile of v1, /device:TPU:8, one launch (start us, length us, event | category | flops | bytes accessed | tf_op | source)
XLA Modules:
  0.0 846.9 jit_solution(2295259165947031657)
XLA Ops:
  7.2 7.7 stack.308
  14.9 9.1 %all-to-all-start = ((bf16[16,32,13824]{2,1,0:T(8,128)(2,1)}), bf16[16,32,13824]{2,1,0:T(8,128)(2,1)}, u32[]{:S(2)}, u32[]{:S(2)}) async-start(bf16[16,32,13824]{2,1,0:T(8,128)(2,1)} %stack.308), calls=%async_computation | async-start | bytes 28311552 | tf_op jit(solution)/shard_map/all_to_all | solution.py:14
  24.2 6.4 collective-permute-start
  30.6 1.3 collective-permute-start.1
  32.0 0.1 fusion.50
  32.6 243.7 %all-reduce.6 = (f32[32]{0:T(128)S(1)}, f32[32]{0:T(128)S(1)}) all-reduce(f32[32]{0:T(128)S(1)} %reduce_sum.183, f32[32]{0:T(128)S(1)} %reduce_sum.181), channel_id=1, replica_groups=mesh['pipe'=2,'slab'=8,'dp'=16] {'slab'}, use_global_device_ids=true, to_apply=%region_5.0 | all-reduce | flops 64 | bytes 512 | tf_op jit(solution)/shard_map/psum | solution.py:126
  276.4 0.6 fusion.146
  277.0 0.4 fusion.6
  277.5 0.7 add_rsqrt_fusion.1
  278.9 0.7 constant_dynamic-update-slice_fusion.26
  279.6 0.6 constant_dynamic-update-slice_fusion.25
  280.2 0.6 constant_dynamic-update-slice_fusion.24
  280.9 0.6 constant_dynamic-update-slice_fusion.23
  281.5 0.6 constant_dynamic-update-slice_fusion.22
  282.2 0.6 constant_dynamic-update-slice_fusion.21
  282.8 0.6 constant_dynamic-update-slice_fusion.20
  283.4 0.6 constant_dynamic-update-slice_fusion.19
  284.1 0.6 constant_dynamic-update-slice_fusion.18
  284.7 0.6 constant_dynamic-update-slice_fusion.17
  285.4 0.6 constant_dynamic-update-slice_fusion.16
  286.0 0.6 constant_dynamic-update-slice_fusion.15
  286.6 0.6 constant_dynamic-update-slice_fusion.14
  287.3 0.6 constant_dynamic-update-slice_fusion.13
  287.9 0.6 constant_dynamic-update-slice_fusion.12
  288.6 0.6 constant_dynamic-update-slice_fusion.11
  289.2 0.6 constant_dynamic-update-slice_fusion.10
  289.9 0.6 constant_dynamic-update-slice_fusion.9
  290.5 0.6 constant_dynamic-update-slice_fusion.8
  291.1 0.6 constant_dynamic-update-slice_fusion.7
  291.8 0.6 constant_dynamic-update-slice_fusion.6
  292.4 0.6 constant_dynamic-update-slice_fusion.5
  293.1 0.6 constant_dynamic-update-slice_fusion.4
  293.7 0.6 constant_dynamic-update-slice_fusion.3
  294.4 0.6 constant_dynamic-update-slice_fusion.2
  295.0 0.6 constant_dynamic-update-slice_fusion.1
  295.7 0.6 constant_dynamic-update-slice_fusion
  296.3 21.1 %reshape_reshape.3 = bf16[512,27,512]{2,1,0:T(8,128)(2,1)} reshape(bf16[16,32,13824]{2,1,0:T(8,128)(2,1)} %all-to-all-done) | data formatting | bytes 28311552 | tf_op jit(solution)/shard_map/reshape;reshape | solution.py:115
  317.4 24.5 %fusion.49 = (f32[512]{0:T(512)S(1)}, f32[512]{0:T(512)S(1)}, f32[512]{0:T(512)S(1)}, f32[512]{0:T(512)S(1)}, f32[2,2,16,512]{3,2,1,0:T(8,128)S(1)}) fusion(f32[512]{0:T(512)S(1)} %sub.59, f32[512]{0:T(512)S(1)} %mul.241, bf16[1,2,1,2,2,16,512]{6,5,4,3,2,1,0:T(8,128)(2,1)S(1)} %copy-done.3, f32[512]{0:T(512)S(1)} %bitcast.568, ...), kind=kOutput, calls=%fused_computation.196 | convolution fusion | flops 906655744 | bytes 16138248 | tf_op jit(solution)/shard_map/tfrwo,oti->frwi/dot_general | solution.py:147
  342.3 28.4 %all-reduce.5 = (f32[32]{0:T(128)S(1)}, f32[32]{0:T(128)S(1)}, f32[32]{0:T(128)S(1)}, f32[32]{0:T(128)S(1)}) all-reduce(f32[32]{0:T(128)S(1)} %reduce_sum.187, f32[32]{0:T(128)S(1)} %reduce_sum.185, f32[32]{0:T(128)S(1)} %reduce_sum.191, f32[32]{0:T(128)S(1)} %reduce_sum.189), channel_id=1, replica_groups=mesh['pipe'=2,'slab'=8,'dp'=16] {'slab'}, use_global_device_ids=true, to_apply=%region_11.12 | all-reduce | flops 128 | bytes 1024 | tf_op jit(solution)/shard_map/psum | solution.py:156
  370.7 0.6 broadcast_divide_fusion.3
  371.8 1.3 collective-permute-start.2
  373.1 1.8 collective-permute-done.2
  374.9 3.2 collective-permute-start.3
  378.2 1.3 collective-permute-start.4
  379.5 0.7 add_rsqrt_fusion
  380.5 8.5 collective-permute-start.5
  388.9 1.5 collective-permute-start.6
  391.2 24.0 %fusion.1 = f32[2,2,16,512,1]{3,2,0,1,4:T(8,128)S(1)} fusion(bf16[512,27,512,1,1]{2,1,0,4,3:T(8,128)(2,1)} %bitcast.559, bf16[27,2,2,16,512]{4,3,2,1,0:T(8,128)(2,1)S(1)} %constant_dynamic-update-slice_fusion.27), kind=kOutput, calls=%fused_computation.2 | convolution fusion | flops 905969664 | bytes 16056320 | tf_op jit(solution)/shard_map/tfrwo,oti->frwi/dot_general | solution.py:147
  415.2 0.1 fusion.76
  415.4 8.5 collective-permute-start.7
  423.8 1.6 collective-permute-start.8
  425.5 8.4 collective-permute-done.8
  435.1 1.7 copy-done.2
  436.8 9.1 %fusion = bf16[512,27,512]{0,2,1:T(8,128)(2,1)} fusion(bf16[27,2,2,2,16,512]{5,4,3,2,1,0:T(8,128)(2,1)} %copy-done.2, bf16[1,2,2,16,512]{4,3,2,1,0:T(8,128)(2,1)S(1)} %bitcast.560, bf16[1,2,2,16,512]{4,3,2,1,0:T(8,128)(2,1)S(1)} %get-tuple-element.43), kind=kOutput, calls=%fused_computation.1 | convolution fusion | flops 1826160640 | bytes 17825792 | tf_op jit(solution)/shard_map/kfrwo,tkfrwi->oti/dot_general | solution.py:178
  445.9 18.6 %copy.72 = bf16[512,13824]{1,0:T(8,128)(2,1)} copy(bf16[512,13824]{0,1:T(8,128)(2,1)} %bitcast.557) | data formatting | bytes 28311552 | tf_op jit(solution)/shard_map/convert_element_type | solution.py:182
  464.6 196.1 %reduce-scatter.2.cloned.1.call-done = bf16[32,13824]{1,0:T(8,128)(2,1)} async-done(((bf16[512,13824]{1,0:T(8,128)(2,1)}), bf16[32,13824]{1,0:T(8,128)(2,1)}) %reduce-scatter.2.cloned.1.call-update) | async-done | bytes 884752 | tf_op jit(solution)/shard_map/reduce_scatter | solution.py:181
  660.7 2.5 bitcast_convert_fusion
  663.6 35.7 %all-reduce.4 = (f32[32]{0:T(128)S(1)}, f32[32]{0:T(128)S(1)}, f32[1,512]{1,0:T(1,128)S(1)}, f32[1,512]{1,0:T(1,128)S(1)}, f32[1,512]{1,0:T(1,128)S(1)}, /*index=5*/f32[1,512]{1,0:T(1,128)S(1)}) all-reduce(f32[32]{0:T(128)S(1)} %reduce_sum.195, f32[32]{0:T(128)S(1)} %reduce_sum.193, ...), channel_id=1, replica_groups=mesh['pipe'=2,'slab'=8,'dp'=16] {'slab'}, use_global_device_ids=true, to_apply=%region_23.24 | all-reduce | flops 2112 | bytes 16896 | tf_op jit(solution)/shard_map/psum | solution.py:156
  699.3 0.6 broadcast_in_dim.47
  699.9 0.6 broadcast_divide_fusion.1
  700.7 0.7 broadcast_divide_fusion
  701.6 0.7 maximum_bitcast_fusion
  702.3 134.9 %all-reduce.9.cloned.1.call-done = f32[1,32,13824]{2,1,0:T(8,128)} async-done(((f32[1,32,13824]{2,1,0:T(8,128)}), f32[1,32,13824]{2,1,0:T(8,128)}) %all-reduce.9.cloned.1.call-update) | async-done | bytes 1769488 | tf_op jit(solution)/shard_map/psum | solution.py:189
  837.3 2.8 copy.189
  (135 shorter events, 5.0 us)
Async XLA Ops:
  7.2 269.8 %copy-start = (bf16[1,1000,1024]{2,1,0:T(8,128)(2,1)S(1)}, bf16[1,1000,1024]{2,1,0:T(8,128)(2,1)}, u32[]{:S(2)}) copy-start(bf16[1,1000,1024]{2,1,0:T(8,128)(2,1)} %param.11) | copy-start | bytes 6144004
  14.9 9.2 %copy-start.4 = (bf16[2,1,2,2,16,512]{5,4,3,2,1,0:T(8,128)(2,1)S(1)}, bf16[2,1,2,2,16,512]{5,4,3,2,1,0:T(8,128)(2,1)}, u32[]{:S(2)}) copy-start(bf16[2,1,2,2,16,512]{5,4,3,2,1,0:T(8,128)(2,1)} %param.8) | copy-start | bytes 393220
  14.9 9.2 %copy-start.5 = (bf16[1,2,2,16,512]{4,3,2,1,0:T(8,128)(2,1)S(1)}, bf16[1,2,2,16,512]{4,3,2,1,0:T(8,128)(2,1)}, u32[]{:S(2)}) copy-start(bf16[1,2,2,16,512]{4,3,2,1,0:T(8,128)(2,1)} %param.9) | copy-start | bytes 196612
  14.9 17.0 %copy-start.6 = (s32[3,1]{0,1:T(1,128)S(1)}, s32[3,1]{0,1:T(1,128)}, u32[]{:S(2)}) copy-start(s32[3,1]{0,1:T(1,128)} %param.13) | copy-start | bytes 40
  14.9 17.1 %copy-start.3 = (bf16[1,2,1,2,2,16,512]{6,5,4,3,2,1,0:T(8,128)(2,1)S(1)}, bf16[1,2,1,2,2,16,512]{6,5,4,3,2,1,0:T(8,128)(2,1)}, u32[]{:S(2)}) copy-start(bf16[1,2,1,2,2,16,512]{6,5,4,3,2,1,0:T(8,128)(2,1)} %param.7) | copy-start | bytes 393220
  14.9 261.4 %copy-start.7 = (s32[3,1]{0,1:T(1,128)S(1)}, s32[3,1]{0,1:T(1,128)}, u32[]{:S(2)}) copy-start(s32[3,1]{0,1:T(1,128)} %param.12) | copy-start | bytes 40
  14.9 281.4 %all-to-all-start = ((bf16[16,32,13824]{2,1,0:T(8,128)(2,1)}), bf16[16,32,13824]{2,1,0:T(8,128)(2,1)}, u32[]{:S(2)}, u32[]{:S(2)}) async-start(bf16[16,32,13824]{2,1,0:T(8,128)(2,1)} %stack.308), calls=%async_computation | async-start | bytes 28311552 | tf_op jit(solution)/shard_map/all_to_all | solution.py:14
  24.1 636.6 %reduce-scatter.2.cloned.1.call-start = ((), (), s32[]{:S(2)}) async-start(), calls=%async_computation.2 | async-start | bytes 15040512 | tf_op jit(solution)/shard_map/reduce_scatter | solution.py:181
  24.2 254.7 %collective-permute-start = (bf16[2,1,16,512]{3,2,1,0:T(8,128)(2,1)S(1)}, bf16[2,1,16,512]{3,2,1,0:T(8,128)(2,1)S(1)}, u32[]{:S(2)}, u32[]{:S(2)}) collective-permute-start(bf16[2,1,16,512]{3,2,1,0:T(8,128)(2,1)S(1)} %get-tuple-element.53), channel_id=1, source_target_pairs={{0,16},{16,32},{32,48},{48,64},{64,80},{80,96},{96,112},{1,17},{17... | collective-permute-start | bytes 98312 | tf_op jit(solution)/shard_map/ppermute | solution.py:28
  30.6 248.3 %collective-permute-start.1 = (bf16[2,1,16,512]{3,2,1,0:T(8,128)(2,1)S(1)}, bf16[2,1,16,512]{3,2,1,0:T(8,128)(2,1)S(1)}, u32[]{:S(2)}, u32[]{:S(2)}) collective-permute-start(bf16[2,1,16,512]{3,2,1,0:T(8,128)(2,1)S(1)} %get-tuple-element.54), channel_id=1, source_target_pairs={{16,0},{32,16},{48,32},{64,48},{80,64},{96,80},{112,96},{17,1},{33... | collective-permute-start | bytes 98312 | tf_op jit(solution)/shard_map/ppermute | solution.py:29
  371.8 3.1 collective-permute-start.2
  374.9 15.5 %collective-permute-start.3 = (bf16[2,1,16,512]{3,2,1,0:T(8,128)(2,1)S(1)}, bf16[2,1,16,512]{3,2,1,0:T(8,128)(2,1)S(1)}, u32[]{:S(2)}, u32[]{:S(2)}) collective-permute-start(bf16[2,1,16,512]{3,2,1,0:T(8,128)(2,1)S(1)} %get-tuple-element.51), channel_id=1, source_target_pairs={{0,16},{16,32},{32,48},{48,64},{64,80},{80,96},{96,112},{1,17},{17... | collective-permute-start | bytes 98312 | tf_op jit(solution)/shard_map/ppermute | solution.py:28
  378.2 12.3 %collective-permute-start.4 = (bf16[2,1,16,512]{3,2,1,0:T(8,128)(2,1)S(1)}, bf16[2,1,16,512]{3,2,1,0:T(8,128)(2,1)S(1)}, u32[]{:S(2)}, u32[]{:S(2)}) collective-permute-start(bf16[2,1,16,512]{3,2,1,0:T(8,128)(2,1)S(1)} %get-tuple-element.52), channel_id=1, source_target_pairs={{16,0},{32,16},{48,32},{64,48},{80,64},{96,80},{112,96},{17,1},{33... | collective-permute-start | bytes 98312 | tf_op jit(solution)/shard_map/ppermute | solution.py:29
  380.5 44.9 %collective-permute-start.5 = (bf16[2,1,16,512]{3,2,1,0:T(8,128)(2,1)S(1)}, bf16[2,1,16,512]{3,2,1,0:T(8,128)(2,1)S(1)}, u32[]{:S(2)}, u32[]{:S(2)}) collective-permute-start(bf16[2,1,16,512]{3,2,1,0:T(8,128)(2,1)S(1)} %get-tuple-element.49), channel_id=1, source_target_pairs={{0,16},{16,32},{32,48},{48,64},{64,80},{80,96},{96,112},{1,17},{17... | collective-permute-start | bytes 98312 | tf_op jit(solution)/shard_map/ppermute | solution.py:28
  388.9 36.5 %collective-permute-start.6 = (bf16[2,1,16,512]{3,2,1,0:T(8,128)(2,1)S(1)}, bf16[2,1,16,512]{3,2,1,0:T(8,128)(2,1)S(1)}, u32[]{:S(2)}, u32[]{:S(2)}) collective-permute-start(bf16[2,1,16,512]{3,2,1,0:T(8,128)(2,1)S(1)} %get-tuple-element.50), channel_id=1, source_target_pairs={{16,0},{32,16},{48,32},{64,48},{80,64},{96,80},{112,96},{17,1},{33... | collective-permute-start | bytes 98312 | tf_op jit(solution)/shard_map/ppermute | solution.py:29
  415.4 10.1 %collective-permute-start.7 = (bf16[2,1,16,512]{3,2,1,0:T(8,128)(2,1)S(1)}, bf16[2,1,16,512]{3,2,1,0:T(8,128)(2,1)S(1)}, u32[]{:S(2)}, u32[]{:S(2)}) collective-permute-start(bf16[2,1,16,512]{3,2,1,0:T(8,128)(2,1)S(1)} %get-tuple-element.47), channel_id=1, source_target_pairs={{0,16},{16,32},{32,48},{48,64},{64,80},{80,96},{96,112},{1,17},{17... | collective-permute-start | bytes 98312 | tf_op jit(solution)/shard_map/ppermute | solution.py:28
  423.8 10.1 %collective-permute-start.8 = (bf16[2,1,16,512]{3,2,1,0:T(8,128)(2,1)S(1)}, bf16[2,1,16,512]{3,2,1,0:T(8,128)(2,1)S(1)}, u32[]{:S(2)}, u32[]{:S(2)}) collective-permute-start(bf16[2,1,16,512]{3,2,1,0:T(8,128)(2,1)S(1)} %get-tuple-element.48), channel_id=1, source_target_pairs={{16,0},{32,16},{48,32},{64,48},{80,64},{96,80},{112,96},{17,1},{33... | collective-permute-start | bytes 98312 | tf_op jit(solution)/shard_map/ppermute | solution.py:29
  435.0 1.7 copy-start.2
  464.6 372.7 %all-reduce.9.cloned.1.call-start = ((), (), s32[]{:S(2)}) async-start(), calls=%async_computation.3 | async-start | bytes 3538944 | tf_op jit(solution)/shard_map/psum | solution.py:189
  701.6 138.4 %copy-start.1 = (bf16[1,1000,1024]{2,1,0:T(8,128)(2,1)S(1)}, bf16[1,1000,1024]{2,1,0:T(8,128)(2,1)}, u32[]{:S(2)}) copy-start(bf16[1,1000,1024]{2,1,0:T(8,128)(2,1)} %param.11) | copy-start | bytes 6144004
Sparse Core Ops, SparseCore 0:
  464.7 195.9 reduce-scatter.1
  663.9 173.2 all-reduce.8
